TPU v7x, 256 devices: a whole 4x4x8 slice. The times are simulated.
256 devices in a mesh: light: 16 (over y, x), depth: 16 (over z, core).
Axes of the slice: x: 4, y: 4, z: 8, core: 2. Of those that a mesh axis runs over, the one named last changes fastest.
Arguments:
- density: float32 [64, 512, 2048], P('light', None, 'depth'), may hold values from 0 to 1
- tf_table: float32 [8, 4, 4], replicated, may hold values from -4.5 to 11
- tf_index: int32 [16, 16], P('light', 'depth'), may hold values from 0 to 7
- light_sources: float32 [2, 512, 2048], P(None, None, 'depth'), may hold values from 0.25 to 2.5
- spread_taps: float32 [9], replicated, may hold values from 0.2 to 1
- view_flip: int32 [32768], P('light'), may hold values from 0 to 1
Outputs:
- image: float32 [4, 32768], P(None, ('light', 'depth'))
All inputs are finite; a program needn't handle non-finite values.
Results may differ from a plain program's by a relative error of at most 0.0003.
Values sent between devices are 32-bit elements; how exact they have to be, the bound alone decides.
A program may use at most 64 MiB of HBM per device.

v0:
```python
import jax
import jax.numpy as jnp
from jax import lax
from jax.sharding import PartitionSpec as P

DEG = 4


AMBIENT = 0.2
LIGHT_DEPTH = 36.0
VIEW_DEPTH = 16.0


def extended_2(shard, sides, width):
    for axis, dim in sides:
        size, length = (lax.axis_size(axis), shard.shape[dim])
        up = [(i, (i + 1) % size) for i in range(size - 1)]
        down = [(j, i) for i, j in up]
        last = lax.slice_in_dim(shard, length - width, length, axis=dim)
        leading = lax.slice_in_dim(shard, 0, width, axis=dim)
        before = lax.ppermute(last, axis, up)
        after = lax.ppermute(leading, axis, down)
        shard = jnp.concatenate([before, shard, after], axis=dim)
    return shard


def shifted(shard, axis, by):
    length = lax.axis_size(axis)
    pairs = [(i, i + by) for i in range(length) if 0 <= i + by < length]
    return lax.ppermute(shard, axis, pairs)


def swapped(block, axis, apart):
    count = lax.axis_size(axis)
    route = []
    for low in range(count):
        high = low | 1 << apart
        if high != low and high < count:
            route += [(low, high), (high, low)]
    return lax.ppermute(block, axis, route)


def spread(plane, weights):
    lead = [(0, 0)] * (plane.ndim - 2)
    rows = plane.shape[-2]
    padded = jnp.pad(plane, lead + [(4, 4), (0, 0)])
    across = weights[0] * padded[..., 0:rows, :]
    for tap in range(1, 9):
        across = across + weights[tap] * padded[..., tap : tap + rows, :]
    cols = plane.shape[-1]
    padded = jnp.pad(across, lead + [(0, 0), (4, 4)])
    result = weights[0] * padded[..., 0:cols]
    for tap in range(1, 9):
        result = result + weights[tap] * padded[..., tap : tap + cols]
    return result


def channel(values, coefs):
    return jax.nn.sigmoid(((coefs[3] * values + coefs[2]) * values + coefs[1]) * values + coefs[0])


def over_blend(front, back):
    colors = front[:3] + jnp.exp(-front[3:4]) * back[:3]
    return jnp.concatenate([colors, front[3:4] + back[3:4]], axis=0)


def per_device(density, tf_table, tf_index, light_sources, spread_taps, view_flip):
    slices, width, cells = density.shape
    n_light = lax.axis_size("light")
    n_depth = lax.axis_size("depth")
    light_pos = lax.axis_index("light")
    depth_pos = lax.axis_index("depth")
    weights = spread_taps / jnp.sum(spread_taps)
    coefs = tf_table[tf_index[0, 0]]
    opacity = channel(density, [coefs[3, k] for k in range(DEG)])
    margin = 4 * slices
    extended = cells + 2 * margin
    opac_ext = extended_2(opacity, (("depth", 2),), margin)
    zpos = depth_pos * cells - margin + jnp.arange(extended, dtype=jnp.int32)
    inside = ((zpos >= 0) & (zpos < n_depth * cells)).astype(jnp.float32)
    fade = jnp.exp(-(LIGHT_DEPTH / (slices * n_light)) * opac_ext) * inside

    def run_slab(ext_buf, reverse):
        seen = []
        for slot in range(slices):
            seen.append(ext_buf[:, margin : margin + cells])
            layer = slices - 1 - slot if reverse else slot
            ext_buf = spread(ext_buf, weights) * fade[layer]
        ordered = seen[::-1] if reverse else seen
        return (ext_buf[:, margin : margin + cells], jnp.stack(ordered))

    def forward_turn(args):
        return run_slab(args[0], False)

    def backward_turn(args):
        return run_slab(args[0], True)

    def waiting(args):
        ext_in, lit_in = args
        return (ext_in[:, margin : margin + cells], lit_in)

    def advance(step, carry):
        buffers, lit = carry
        ext_bufs = extended_2(buffers, (("depth", 2),), margin)
        mine_fwd = light_pos == step
        mine_bwd = light_pos == n_light - 1 - step
        leave_fwd, lit_fwd = lax.cond(mine_fwd, forward_turn, waiting, (ext_bufs[0], lit[0]))
        leave_bwd, lit_bwd = lax.cond(mine_bwd, backward_turn, waiting, (ext_bufs[1], lit[1]))
        sent_fwd = shifted(leave_fwd, "light", 1)
        sent_bwd = shifted(leave_bwd, "light", -1)
        return (jnp.stack([sent_fwd, sent_bwd]), jnp.stack([lit_fwd, lit_bwd]))

    lit_zero = jnp.zeros((2, slices, width, cells), jnp.float32)
    _, lit = lax.fori_loop(0, n_light, advance, (light_sources, lit_zero))
    pixels = slices * width
    flip_rows = view_flip != 0
    tau = (VIEW_DEPTH / (n_depth * cells) * opacity).reshape(pixels, cells)
    upper = (jnp.arange(cells)[:, None] <= jnp.arange(cells)[None, :]).astype(jnp.float32)
    cum = jnp.dot(tau, upper, precision=lax.Precision.HIGHEST, preferred_element_type=jnp.float32)
    total = jnp.sum(tau, axis=1)
    before = jnp.where(flip_rows[:, None], total[:, None] - cum, cum - tau)
    lighting = (AMBIENT + lit[0] + lit[1]).reshape(pixels, cells)
    trans = jnp.exp(-before) * lighting * (1.0 - jnp.exp(-tau))
    flat = density.reshape(pixels, cells)
    planes = [
        jnp.sum(trans * channel(flat, [coefs[kind, k] for k in range(DEG)]), axis=1)
        for kind in range(3)
    ]
    partial_img = jnp.stack(planes + [total])
    block = pixels // n_depth
    nbits = n_depth.bit_length() - 1
    current = partial_img.reshape((4,) + (2,) * nbits + (block,))
    flip_parts = flip_rows.reshape((2,) * nbits + (block,))
    for bit in range(nbits):
        place = nbits - bit
        my_bit = depth_pos >> bit & 1
        keep = lax.dynamic_index_in_dim(current, my_bit, place, keepdims=False)
        send = lax.dynamic_index_in_dim(current, 1 - my_bit, place, keepdims=False)
        flip_parts = lax.dynamic_index_in_dim(flip_parts, my_bit, place - 1, keepdims=False)
        other = swapped(send, "depth", bit)
        me_front = (my_bit == 0) == jnp.logical_not(flip_parts)
        front = jnp.where(me_front[None], keep, other)
        back = jnp.where(me_front[None], other, keep)
        current = over_blend(front, back)
    return jnp.concatenate([current[:3], 1.0 - jnp.exp(-current[3:4])], axis=0)


def solution(mesh):
    placed = (
        P("light", None, "depth"),
        P(),
        P("light", "depth"),
        P(None, None, "depth"),
        P(),
        P("light"),
    )
    return jax.shard_map(
        per_device,
        mesh=mesh,
        in_specs=placed,
        out_specs=P(None, ("light", "depth")),
        check_vma=False,
    )
```

profile of v0, /device:TPU:62, one launch (start us, length us, event | category | flops | bytes accessed | tf_op | source)
XLA Modules:
  0.0 1452.8 jit_solution(3027562817716594610)
XLA Ops:
  25.6 1394.5 %while.15 = (s32[]{:T(128)}, f32[2,512,128]{2,1,0:T(8,128)S(1)}, f32[2,4,512,128]{3,2,1,0:T(8,128)}, s32[]{:T(128)}, f32[9]{0:T(128)S(1)}, /*index=5*/f32[4,512,160]{2,1,0:T(8,128)S(1)}, s32[]{:T(128)}, s32[]{:T(128)}) while((s32[]{:T(128)}, f32[2,512,128]{2,1,0:T(8,128)S(1)}, f32[2,4,512,128]{3,2,1,0:T(8,128)}, s32[]{:T(128)}, ...), condition=%wide.region_7.8_spmd, body=%wide.region_2.7_spmd.sunk | while | flops 25493512 | bytes 51119308 | solution.py:114
  42.3 52.6 %conditional.4 = (f32[512,160]{1,0:T(8,128)S(1)}, f32[1,4,512,128]{3,2,1,0:T(8,128)S(1)}) conditional(s32[]{:T(128)} %convert_element_type.44, (f32[2,4,512,128]{3,2,1,0:T(8,128)S(1)}, f32[512,160]{1,0:T(8,128)S(1)}) %tuple.127, (f32[9]{0:T(128)S(1)}, f32[512,160]{1,0:T(8,128)S(1)}, f32[4,512,160]{2,1,0:T(8,128)S(1)}) %tuple.116), branch_computations={%region_5.5_spmd, %region_6.6_spmd} | conditional | flops 12255232 | bytes 10748280 | solution.py:108
  49.2 6.7 bitcast_multiply_fusion.7
  62.0 6.7 bitcast_multiply_fusion.6
  74.9 6.7 bitcast_multiply_fusion.5
  87.9 6.7 bitcast_multiply_fusion.4
  125.8 53.9 %collective-permute-start.2 = (f32[512,128]{1,0:T(8,128)S(1)}, f32[512,128]{1,0:T(8,128)S(1)}, u32[]{:S(2)}, u32[]{:S(2)}) collective-permute-start(f32[512,128]{1,0:T(8,128)S(1)} %slice.1328), channel_id=1, source_target_pairs={{16,0},{32,16},{48,32},{64,48},{80,64},{96,80},{112,96},{128,112},... | collective-permute-start | bytes 786440 | tf_op jit(solution)/shard_map/while/body/eval_jaxpr/ppermute | solution.py:30
  217.8 55.7 %collective-permute-done.3 = f32[512,128]{1,0:T(8,128)S(1)} collective-permute-done((f32[512,128]{1,0:T(8,128)S(1)}, f32[512,128]{1,0:T(8,128)S(1)}, u32[]{:S(2)}, u32[]{:S(2)}) %collective-permute-start.3) | collective-permute-done | bytes 262176 | tf_op jit(solution)/shard_map/while/body/eval_jaxpr/ppermute | solution.py:30
  324.7 52.5 %collective-permute-start.2 = (f32[512,128]{1,0:T(8,128)S(1)}, f32[512,128]{1,0:T(8,128)S(1)}, u32[]{:S(2)}, u32[]{:S(2)}) collective-permute-start(f32[512,128]{1,0:T(8,128)S(1)} %slice.1328), channel_id=1, source_target_pairs={{16,0},{32,16},{48,32},{64,48},{80,64},{96,80},{112,96},{128,112},... | collective-permute-start | bytes 786440 | tf_op jit(solution)/shard_map/while/body/eval_jaxpr/ppermute | solution.py:30
  418.6 56.5 %collective-permute-done.3 = f32[512,128]{1,0:T(8,128)S(1)} collective-permute-done((f32[512,128]{1,0:T(8,128)S(1)}, f32[512,128]{1,0:T(8,128)S(1)}, u32[]{:S(2)}, u32[]{:S(2)}) %collective-permute-start.3) | collective-permute-done | bytes 262176 | tf_op jit(solution)/shard_map/while/body/eval_jaxpr/ppermute | solution.py:30
  528.3 50.4 %collective-permute-start.2 = (f32[512,128]{1,0:T(8,128)S(1)}, f32[512,128]{1,0:T(8,128)S(1)}, u32[]{:S(2)}, u32[]{:S(2)}) collective-permute-start(f32[512,128]{1,0:T(8,128)S(1)} %slice.1328), channel_id=1, source_target_pairs={{16,0},{32,16},{48,32},{64,48},{80,64},{96,80},{112,96},{128,112},... | collective-permute-start | bytes 786440 | tf_op jit(solution)/shard_map/while/body/eval_jaxpr/ppermute | solution.py:30
  620.7 51.8 %collective-permute-done.3 = f32[512,128]{1,0:T(8,128)S(1)} collective-permute-done((f32[512,128]{1,0:T(8,128)S(1)}, f32[512,128]{1,0:T(8,128)S(1)}, u32[]{:S(2)}, u32[]{:S(2)}) %collective-permute-start.3) | collective-permute-done | bytes 262176 | tf_op jit(solution)/shard_map/while/body/eval_jaxpr/ppermute | solution.py:30
  724.8 50.4 %collective-permute-start.2 = (f32[512,128]{1,0:T(8,128)S(1)}, f32[512,128]{1,0:T(8,128)S(1)}, u32[]{:S(2)}, u32[]{:S(2)}) collective-permute-start(f32[512,128]{1,0:T(8,128)S(1)} %slice.1328), channel_id=1, source_target_pairs={{16,0},{32,16},{48,32},{64,48},{80,64},{96,80},{112,96},{128,112},... | collective-permute-start | bytes 786440 | tf_op jit(solution)/shard_map/while/body/eval_jaxpr/ppermute | solution.py:30
  816.9 106.5 %collective-permute-done.3 = f32[512,128]{1,0:T(8,128)S(1)} collective-permute-done((f32[512,128]{1,0:T(8,128)S(1)}, f32[512,128]{1,0:T(8,128)S(1)}, u32[]{:S(2)}, u32[]{:S(2)}) %collective-permute-start.3) | collective-permute-done | bytes 262176 | tf_op jit(solution)/shard_map/while/body/eval_jaxpr/ppermute | solution.py:30
  940.8 57.3 %collective-permute-start.2 = (f32[512,128]{1,0:T(8,128)S(1)}, f32[512,128]{1,0:T(8,128)S(1)}, u32[]{:S(2)}, u32[]{:S(2)}) collective-permute-start(f32[512,128]{1,0:T(8,128)S(1)} %slice.1328), channel_id=1, source_target_pairs={{16,0},{32,16},{48,32},{64,48},{80,64},{96,80},{112,96},{128,112},... | collective-permute-start | bytes 786440 | tf_op jit(solution)/shard_map/while/body/eval_jaxpr/ppermute | solution.py:30
  1004.8 56.4 %collective-permute-done.3 = f32[512,128]{1,0:T(8,128)S(1)} collective-permute-done((f32[512,128]{1,0:T(8,128)S(1)}, f32[512,128]{1,0:T(8,128)S(1)}, u32[]{:S(2)}, u32[]{:S(2)}) %collective-permute-start.3) | collective-permute-done | bytes 262176 | tf_op jit(solution)/shard_map/while/body/eval_jaxpr/ppermute | solution.py:30
  1078.6 54.9 %collective-permute-start.2 = (f32[512,128]{1,0:T(8,128)S(1)}, f32[512,128]{1,0:T(8,128)S(1)}, u32[]{:S(2)}, u32[]{:S(2)}) collective-permute-start(f32[512,128]{1,0:T(8,128)S(1)} %slice.1328), channel_id=1, source_target_pairs={{16,0},{32,16},{48,32},{64,48},{80,64},{96,80},{112,96},{128,112},... | collective-permute-start | bytes 786440 | tf_op jit(solution)/shard_map/while/body/eval_jaxpr/ppermute | solution.py:30
  1140.2 56.4 %collective-permute-done.3 = f32[512,128]{1,0:T(8,128)S(1)} collective-permute-done((f32[512,128]{1,0:T(8,128)S(1)}, f32[512,128]{1,0:T(8,128)S(1)}, u32[]{:S(2)}, u32[]{:S(2)}) %collective-permute-start.3) | collective-permute-done | bytes 262176 | tf_op jit(solution)/shard_map/while/body/eval_jaxpr/ppermute | solution.py:30
  1214.0 57.0 %collective-permute-start.2 = (f32[512,128]{1,0:T(8,128)S(1)}, f32[512,128]{1,0:T(8,128)S(1)}, u32[]{:S(2)}, u32[]{:S(2)}) collective-permute-start(f32[512,128]{1,0:T(8,128)S(1)} %slice.1328), channel_id=1, source_target_pairs={{16,0},{32,16},{48,32},{64,48},{80,64},{96,80},{112,96},{128,112},... | collective-permute-start | bytes 786440 | tf_op jit(solution)/shard_map/while/body/eval_jaxpr/ppermute | solution.py:30
  1277.7 56.4 %collective-permute-done.3 = f32[512,128]{1,0:T(8,128)S(1)} collective-permute-done((f32[512,128]{1,0:T(8,128)S(1)}, f32[512,128]{1,0:T(8,128)S(1)}, u32[]{:S(2)}, u32[]{:S(2)}) %collective-permute-start.3) | collective-permute-done | bytes 262176 | tf_op jit(solution)/shard_map/while/body/eval_jaxpr/ppermute | solution.py:30
  1355.2 52.6 %conditional.5 = (f32[512,160]{1,0:T(8,128)S(1)}, f32[1,4,512,128]{3,2,1,0:T(8,128)S(1)}) conditional(s32[]{:T(128)} %convert_element_type.45, (f32[2,4,512,128]{3,2,1,0:T(8,128)}, f32[512,160]{1,0:T(8,128)S(1)}) %tuple.117, (f32[9]{0:T(128)S(1)}, f32[512,160]{1,0:T(8,128)S(1)}, f32[4,512,160]{2,1,0:T(8,128)S(1)}) %tuple.118), branch_computations={%region_3.3_spmd, %region_4.4_spmd} | conditional | flops 12255232 | bytes 10748280 | solution.py:107
  1362.0 6.7 bitcast_multiply_fusion.3
  1375.1 6.7 bitcast_multiply_fusion.2
  1423.3 10.9 multiply_reduce_fusion.2
  (512 shorter events, 602.4 us)
Async XLA Ops:
  9.0 11.9 collective-permute-start.5
  29.9 10.8 collective-permute-start.1
  113.2 10.8 collective-permute-start.1
  125.8 60.6 %collective-permute-start.2 = (f32[512,128]{1,0:T(8,128)S(1)}, f32[512,128]{1,0:T(8,128)S(1)}, u32[]{:S(2)}, u32[]{:S(2)}) collective-permute-start(f32[512,128]{1,0:T(8,128)S(1)} %slice.1328), channel_id=1, source_target_pairs={{16,0},{32,16},{48,32},{64,48},{80,64},{96,80},{112,96},{128,112},... | collective-permute-start | bytes 786440 | tf_op jit(solution)/shard_map/while/body/eval_jaxpr/ppermute | solution.py:30
  196.3 10.8 collective-permute-start.1
  213.5 60.1 %collective-permute-start.3 = (f32[512,128]{1,0:T(8,128)S(1)}, f32[512,128]{1,0:T(8,128)S(1)}, u32[]{:S(2)}, u32[]{:S(2)}) collective-permute-start(f32[512,128]{1,0:T(8,128)S(1)} %slice.1329), channel_id=1, source_target_pairs={{0,16},{16,32},{32,48},{48,64},{64,80},{80,96},{96,112},{112,128},... | collective-permute-start | bytes 786440 | tf_op jit(solution)/shard_map/while/body/eval_jaxpr/ppermute | solution.py:30
  324.7 59.2 %collective-permute-start.2 = (f32[512,128]{1,0:T(8,128)S(1)}, f32[512,128]{1,0:T(8,128)S(1)}, u32[]{:S(2)}, u32[]{:S(2)}) collective-permute-start(f32[512,128]{1,0:T(8,128)S(1)} %slice.1328), channel_id=1, source_target_pairs={{16,0},{32,16},{48,32},{64,48},{80,64},{96,80},{112,96},{128,112},... | collective-permute-start | bytes 786440 | tf_op jit(solution)/shard_map/while/body/eval_jaxpr/ppermute | solution.py:30
  407.6 11.0 collective-permute-start.2
  414.2 60.8 %collective-permute-start.3 = (f32[512,128]{1,0:T(8,128)S(1)}, f32[512,128]{1,0:T(8,128)S(1)}, u32[]{:S(2)}, u32[]{:S(2)}) collective-permute-start(f32[512,128]{1,0:T(8,128)S(1)} %slice.1329), channel_id=1, source_target_pairs={{0,16},{16,32},{32,48},{48,64},{64,80},{80,96},{96,112},{112,128},... | collective-permute-start | bytes 786440 | tf_op jit(solution)/shard_map/while/body/eval_jaxpr/ppermute | solution.py:30
  492.5 12.4 collective-permute-start.2
  528.3 57.1 %collective-permute-start.2 = (f32[512,128]{1,0:T(8,128)S(1)}, f32[512,128]{1,0:T(8,128)S(1)}, u32[]{:S(2)}, u32[]{:S(2)}) collective-permute-start(f32[512,128]{1,0:T(8,128)S(1)} %slice.1328), channel_id=1, source_target_pairs={{16,0},{32,16},{48,32},{64,48},{80,64},{96,80},{112,96},{128,112},... | collective-permute-start | bytes 786440 | tf_op jit(solution)/shard_map/while/body/eval_jaxpr/ppermute | solution.py:30
  608.3 12.4 collective-permute-start.2
  616.4 56.2 %collective-permute-start.3 = (f32[512,128]{1,0:T(8,128)S(1)}, f32[512,128]{1,0:T(8,128)S(1)}, u32[]{:S(2)}, u32[]{:S(2)}) collective-permute-start(f32[512,128]{1,0:T(8,128)S(1)} %slice.1329), channel_id=1, source_target_pairs={{0,16},{16,32},{32,48},{48,64},{64,80},{80,96},{96,112},{112,128},... | collective-permute-start | bytes 786440 | tf_op jit(solution)/shard_map/while/body/eval_jaxpr/ppermute | solution.py:30
  690.0 12.4 collective-permute-start.2
  724.8 57.1 %collective-permute-start.2 = (f32[512,128]{1,0:T(8,128)S(1)}, f32[512,128]{1,0:T(8,128)S(1)}, u32[]{:S(2)}, u32[]{:S(2)}) collective-permute-start(f32[512,128]{1,0:T(8,128)S(1)} %slice.1328), channel_id=1, source_target_pairs={{16,0},{32,16},{48,32},{64,48},{80,64},{96,80},{112,96},{128,112},... | collective-permute-start | bytes 786440 | tf_op jit(solution)/shard_map/while/body/eval_jaxpr/ppermute | solution.py:30
  804.4 12.4 collective-permute-start.2
  812.5 110.9 %collective-permute-start.3 = (f32[512,128]{1,0:T(8,128)S(1)}, f32[512,128]{1,0:T(8,128)S(1)}, u32[]{:S(2)}, u32[]{:S(2)}) collective-permute-start(f32[512,128]{1,0:T(8,128)S(1)} %slice.1329), channel_id=1, source_target_pairs={{0,16},{16,32},{32,48},{48,64},{64,80},{80,96},{96,112},{112,128},... | collective-permute-start | bytes 786440 | tf_op jit(solution)/shard_map/while/body/eval_jaxpr/ppermute | solution.py:30
  940.8 64.0 %collective-permute-start.2 = (f32[512,128]{1,0:T(8,128)S(1)}, f32[512,128]{1,0:T(8,128)S(1)}, u32[]{:S(2)}, u32[]{:S(2)}) collective-permute-start(f32[512,128]{1,0:T(8,128)S(1)} %slice.1328), channel_id=1, source_target_pairs={{16,0},{32,16},{48,32},{64,48},{80,64},{96,80},{112,96},{128,112},... | collective-permute-start | bytes 786440 | tf_op jit(solution)/shard_map/while/body/eval_jaxpr/ppermute | solution.py:30
  1000.5 60.7 %collective-permute-start.3 = (f32[512,128]{1,0:T(8,128)S(1)}, f32[512,128]{1,0:T(8,128)S(1)}, u32[]{:S(2)}, u32[]{:S(2)}) collective-permute-start(f32[512,128]{1,0:T(8,128)S(1)} %slice.1329), channel_id=1, source_target_pairs={{0,16},{16,32},{32,48},{48,64},{64,80},{80,96},{96,112},{112,128},... | collective-permute-start | bytes 786440 | tf_op jit(solution)/shard_map/while/body/eval_jaxpr/ppermute | solution.py:30
  1078.6 61.6 %collective-permute-start.2 = (f32[512,128]{1,0:T(8,128)S(1)}, f32[512,128]{1,0:T(8,128)S(1)}, u32[]{:S(2)}, u32[]{:S(2)}) collective-permute-start(f32[512,128]{1,0:T(8,128)S(1)} %slice.1328), channel_id=1, source_target_pairs={{16,0},{32,16},{48,32},{64,48},{80,64},{96,80},{112,96},{128,112},... | collective-permute-start | bytes 786440 | tf_op jit(solution)/shard_map/while/body/eval_jaxpr/ppermute | solution.py:30
  1135.9 60.7 %collective-permute-start.3 = (f32[512,128]{1,0:T(8,128)S(1)}, f32[512,128]{1,0:T(8,128)S(1)}, u32[]{:S(2)}, u32[]{:S(2)}) collective-permute-start(f32[512,128]{1,0:T(8,128)S(1)} %slice.1329), channel_id=1, source_target_pairs={{0,16},{16,32},{32,48},{48,64},{64,80},{80,96},{96,112},{112,128},... | collective-permute-start | bytes 786440 | tf_op jit(solution)/shard_map/while/body/eval_jaxpr/ppermute | solution.py:30
  1214.0 63.7 %collective-permute-start.2 = (f32[512,128]{1,0:T(8,128)S(1)}, f32[512,128]{1,0:T(8,128)S(1)}, u32[]{:S(2)}, u32[]{:S(2)}) collective-permute-start(f32[512,128]{1,0:T(8,128)S(1)} %slice.1328), channel_id=1, source_target_pairs={{16,0},{32,16},{48,32},{64,48},{80,64},{96,80},{112,96},{128,112},... | collective-permute-start | bytes 786440 | tf_op jit(solution)/shard_map/while/body/eval_jaxpr/ppermute | solution.py:30
  1273.4 60.7 %collective-permute-start.3 = (f32[512,128]{1,0:T(8,128)S(1)}, f32[512,128]{1,0:T(8,128)S(1)}, u32[]{:S(2)}, u32[]{:S(2)}) collective-permute-start(f32[512,128]{1,0:T(8,128)S(1)} %slice.1329), channel_id=1, source_target_pairs={{0,16},{16,32},{32,48},{48,64},{64,80},{80,96},{96,112},{112,128},... | collective-permute-start | bytes 786440 | tf_op jit(solution)/shard_map/while/body/eval_jaxpr/ppermute | solution.py:30
  1351.5 61.6 %collective-permute-start.2 = (f32[512,128]{1,0:T(8,128)S(1)}, f32[512,128]{1,0:T(8,128)S(1)}, u32[]{:S(2)}, u32[]{:S(2)}) collective-permute-start(f32[512,128]{1,0:T(8,128)S(1)} %slice.1328), channel_id=1, source_target_pairs={{16,0},{32,16},{48,32},{64,48},{80,64},{96,80},{112,96},{128,112},... | collective-permute-start | bytes 786440 | tf_op jit(solution)/shard_map/while/body/eval_jaxpr/ppermute | solution.py:30
  (121 other events, 1085.0 us)
where the time goes:
time: 1460 us; the launch traced here: 1450 us
  waiting for transfers between devices  633 us (43%)
  starting transfers between devices  517 us (35%)
  other arithmetic  203 us (14%)
  local copies, waits for them, and re-layouts  84.9 us (6%)
    ppermute x32, waiting for transfers between devices, shifted(): return lax.ppermute(shard, axis, pairs)  489 us
    ppermute x32, starting transfers between devices, shifted(): return lax.ppermute(shard, axis, pairs)  435 us
    ppermute x17, waiting for transfers between devices, extended_2(): after = lax.ppermute(leading, axis, down)  73.1 us
    another operation x34, other arithmetic, advance(): return (jnp.stack([sent_fwd, sent_bwd]), jnp.stack([lit_fwd, lit_bwd]))  64.7 us
    ppermute x17, waiting for transfers between devices, extended_2(): before = lax.ppermute(last, axis, up)  61.2 us
    mul x8, other arithmetic, run_slab(): ext_buf = spread(ext_buf, weights) * fade[layer]  53.8 us
    add x8, other arithmetic, spread(): across = across + weights[tap] * padded[..., tap:tap + rows, :]  48.9 us
    ppermute x17, starting transfers between devices, extended_2(): before = lax.ppermute(last, axis, up)  40.7 us
  transfers between devices with their start and end apart: 70, of which 52 were waited for; matrix products, arithmetic and copies ran while one was open for 9% of the time, Pallas kernels for 0%

commit v1 on v0

v1 whole, which is shorter than its diff:
```python
import functools

import jax
import jax.numpy as jnp
from jax import lax
from jax.experimental import pallas as pl
from jax.experimental.pallas import tpu as pltpu
from jax.sharding import PartitionSpec as P

AMBIENT = 0.2
LIGHT_DEPTH = 36.0
VIEW_DEPTH = 16.0

SL = 4
ROWS = 512
LANES = 128
CH = 32
NCH = 17
PAD = 32
TALL = PAD + NCH * CH
FCH = 64
NF = ROWS // FCH
BLOCKS = SL * ROWS // LANES
MESH = pl.DeviceIdType.MESH


def channel(v, c):
    return jax.nn.sigmoid(((c[3] * v + c[2]) * v + c[1]) * v + c[0])


def kernel(
    nl,
    nd,
    dens,
    table,
    index,
    sources,
    taps,
    flips,
    out,
    lev,
    leave,
    fade,
    fade_nb,
    light_nb,
    weight,
    totals,
    gathered,
    part,
    parts,
    s_main,
    r_main,
    s_nb,
    r_nb,
    s_fade,
    r_fade,
    s_tot,
    r_tot,
    s_part,
    r_part,
):
    l = lax.axis_index("light")
    d = lax.axis_index("depth")
    has_left = d > 0
    has_right = d < nd - 1
    mine = BLOCKS // nd
    f32 = jnp.float32

    zeros = jnp.zeros((PAD, LANES), f32)
    for way in range(2):
        for s in range(SL):
            for tile in range(2):
                lev[way, s, tile, 0:PAD, :] = zeros
        for tile in range(2):
            lev[way, 0, tile, PAD + ROWS : TALL, :] = zeros
    for x in range(SL):
        fade[x, 0:PAD, :] = zeros
        fade[x, PAD + ROWS : TALL, :] = zeros
        for side in range(2):
            fade_nb[side, x, 0:PAD, :] = zeros
            fade_nb[side, x, PAD + ROWS : TALL, :] = zeros
    for side, there in ((0, has_left), (1, has_right)):

        @pl.when(jnp.logical_not(there))
        def _():
            @pl.loop(0, ROWS // CH)
            def _(i):
                at = pl.ds(pl.multiple_of(PAD + i * CH, CH), CH)
                for x in range(SL):
                    fade_nb[side, x, at, :] = zeros
                for way in range(2):
                    light_nb[way, side, at, :] = zeros

    for way, first in ((0, 0), (1, nl - 1)):

        @pl.when(l == first)
        def _():
            @pl.loop(0, ROWS // CH)
            def _(i):
                lev[way, 0, 0, pl.ds(pl.multiple_of(PAD + i * CH, CH), CH), :] = sources[
                    way, pl.ds(pl.multiple_of(i * CH, CH), CH), :
                ]

    barrier = pltpu.get_barrier_semaphore()

    def greet(to_l, to_d):
        pl.semaphore_signal(barrier, 1, device_id=(to_l, to_d), device_id_type=MESH)

    @pl.loop(1, nd)
    def _(j):
        greet(l, lax.rem(d + j, nd))

    for dl in (-1, 1):
        near = (l + dl >= 0) & (l + dl < nl)
        for dd in (-1, 0, 1):

            @pl.when(near & (d + dd >= 0) & (d + dd < nd))
            def _():
                greet(l + dl, d + dd)

    k_at = index[0, 0]
    coef = [[table[k_at, k, j] for j in range(4)] for k in range(4)]
    absorb = LIGHT_DEPTH / (SL * nl)
    thick = VIEW_DEPTH / (nd * LANES)

    @pl.loop(0, NF)
    def _(i):
        src = pl.ds(pl.multiple_of(i * FCH, FCH), FCH)
        dst = pl.ds(pl.multiple_of(PAD + i * FCH, 32), FCH)
        for x in range(SL):
            fade[x, dst, :] = jnp.exp(-absorb * channel(dens[x, src, :], coef[3]))

    beside = (has_left.astype(jnp.int32) + has_right.astype(jnp.int32)) + 1
    lights = (l > 0).astype(jnp.int32) + (l < nl - 1).astype(jnp.int32)
    pl.semaphore_wait(barrier, nd - 1 + lights * beside)

    def fade_copy(side, i):
        rows = pl.ds(pl.multiple_of(PAD + i * FCH, 32), FCH)
        to = d - 1 + 2 * side
        return pltpu.make_async_remote_copy(
            src_ref=fade.at[:, rows, :],
            dst_ref=fade_nb.at[1 - side, :, rows, :],
            send_sem=s_fade.at[side, i],
            recv_sem=r_fade.at[1 - side, i],
            device_id=(l, to),
            device_id_type=MESH,
        )

    def source_copy(way, side, j):
        return pltpu.make_async_remote_copy(
            src_ref=sources.at[way, pl.ds(pl.multiple_of(j * CH, CH), CH), :],
            dst_ref=light_nb.at[way, 1 - side, pl.ds(pl.multiple_of(PAD + j * CH, CH), CH), :],
            send_sem=s_nb.at[way, side, j],
            recv_sem=r_nb.at[way, 1 - side, j],
            device_id=(l, d - 1 + 2 * side),
            device_id_type=MESH,
        )

    sides = ((0, has_left), (1, has_right))

    @pl.loop(0, NF)
    def _(i):
        for side, there in sides:
            for way, first in ((0, 0), (1, nl - 1)):

                @pl.when(there & (l == first))
                def _():
                    source_copy(way, side, 2 * i).start()
                    source_copy(way, side, 2 * i + 1).start()

            @pl.when(there)
            def _():
                fade_copy(side, i).start()

    total_tap = taps[0]
    for t in range(1, 9):
        total_tap = total_tap + taps[t]
    total_vec = jnp.full((8, LANES), total_tap, f32)
    tap = [(jnp.full((8, LANES), taps[t], f32) / total_vec)[0:1, :] for t in range(9)]
    lane = lax.broadcasted_iota(jnp.int32, (CH, LANES), 1)
    low_half = lane < LANES // 2

    def hops(way):
        return l + way * (nl - 1 - 2 * l)

    def rows_out(way, i):
        n = hops(way)
        return pl.ds(pl.multiple_of(PAD - 16 + i * CH - 16 * lax.rem(n, 2), 16), CH)

    def main_copy(way, i):
        rows = rows_out(way, i)
        return pltpu.make_async_remote_copy(
            src_ref=leave.at[way, :, rows, :],
            dst_ref=lev.at[way, 0, :, rows, :],
            send_sem=s_main.at[way, i],
            recv_sem=r_main.at[way, i - lax.rem(hops(way), 2)],
            device_id=(l + 1 - 2 * way, d),
            device_id_type=MESH,
        )

    def side_copy(way, side, i):
        rows = rows_out(way, i)
        return pltpu.make_async_remote_copy(
            src_ref=leave.at[way, 0, rows, :],
            dst_ref=light_nb.at[way, 1 - side, rows, :],
            send_sem=s_nb.at[way, side, i],
            recv_sem=r_nb.at[way, 1 - side, i - 1],
            device_id=(l + 1 - 2 * way, d - 1 + 2 * side),
            device_id_type=MESH,
        )

    def wait_recv(dst, sem):
        pltpu.make_async_copy(dst, dst, sem).wait()

    def step(way, i, lead):
        n = hops(way)
        odd = lax.rem(n, 2)
        base = pl.multiple_of(PAD + i * CH - 16 * odd, 16)
        rows = pl.ds(base, CH)

        for side, there in sides:

            @pl.when(there & lead & (lax.rem(i, 2) == 0) & (i < 2 * NF))
            def _():
                at = pl.ds(pl.multiple_of(PAD + i * CH, CH), FCH)
                wait_recv(fade_nb.at[side, :, at, :], r_fade.at[side, lax.div(i, 2)])

        @pl.when((n > 0) & (i < NCH - 1 + odd))
        def _():
            wait_recv(lev.at[way, 0, :, rows, :], r_main.at[way, i])

        @pl.when((lax.rem(n, 4) == 0) & (i < NCH - 1))
        def _():
            for side, there in sides:

                @pl.when(there)
                def _():
                    wait_recv(light_nb.at[way, side, rows, :], r_nb.at[way, side, i])

            lev[way, 0, 1, rows, :] = jnp.where(
                low_half, light_nb[way, 1, rows, :], light_nb[way, 0, rows, :]
            )

        for s in range(SL):
            layer = s + way * (SL - 1 - 2 * s)
            cols = []
            for tile in range(2):
                acc = tap[0] * lev[way, s, tile, pl.ds(base - 8, CH), :]
                for t in range(1, 9):
                    acc = acc + tap[t] * lev[way, s, tile, pl.ds(base - 8 + t, CH), :]
                cols.append(acc)
            a, b = cols
            sum_a, sum_b = tap[4] * a, tap[4] * b
            for t in range(9):
                by = t - 4
                if by == 0:
                    continue
                ra = pltpu.roll(a, (-by) % LANES, 1)
                rb = pltpu.roll(b, (-by) % LANES, 1)
                own = lane < LANES - by if by > 0 else lane >= -by
                sum_a = sum_a + tap[t] * jnp.where(own, ra, rb)
                sum_b = sum_b + tap[t] * jnp.where(own, rb, ra)
            there_rows = pl.ds(base - 4 * (s + 1), CH)
            fade_a = fade[layer, there_rows, :]
            fade_b = jnp.where(
                low_half, fade_nb[1, layer, there_rows, :], fade_nb[0, layer, there_rows, :]
            )
            if s < SL - 1:
                lev[way, s + 1, 0, rows, :] = sum_a * fade_a
                lev[way, s + 1, 1, rows, :] = sum_b * fade_b
            else:
                leave[way, 0, rows_out(way, i), :] = sum_a * fade_a
                leave[way, 1, rows_out(way, i), :] = sum_b * fade_b

        @pl.when((n < nl - 1) & (i >= odd))
        def _():
            main_copy(way, i).start()
            for side, there in sides:

                @pl.when(there & (lax.rem(n, 4) == 3))
                def _():
                    side_copy(way, side, i).start()

    row_i = lax.broadcasted_iota(jnp.int32, (LANES, LANES), 0)
    lane_i = lax.broadcasted_iota(jnp.int32, (LANES, LANES), 1)

    def compact(column):
        return jnp.sum(jnp.where(row_i == lane_i, column, 0.0), axis=0, keepdims=True)

    def total_copy(j):
        peer = lax.rem(d + j, nd)
        return pltpu.make_async_remote_copy(
            src_ref=totals,
            dst_ref=gathered.at[d],
            send_sem=s_tot.at[j],
            recv_sem=r_tot.at[d],
            device_id=(l, peer),
            device_id_type=MESH,
        )

    def prepare():
        earlier = (row_i < lane_i).astype(f32)
        later = (row_i > lane_i).astype(f32)

        @pl.loop(0, BLOCKS)
        def _(b):
            x = lax.div(b, SL)
            at = pl.ds(pl.multiple_of(lax.rem(b, SL) * LANES, LANES), LANES)
            v = dens[x, at, :]
            tau = thick * channel(v, coef[3])
            front = jnp.dot(tau, earlier, precision=lax.Precision.HIGHEST, preferred_element_type=f32)
            back = jnp.dot(tau, later, precision=lax.Precision.HIGHEST, preferred_element_type=f32)
            flip = jnp.broadcast_to(flips[pl.ds(b, 1), :].astype(f32), (LANES, LANES)).T
            before = jnp.where(flip != 0.0, back, front)
            common = jnp.exp(-before) * (1.0 - jnp.exp(-tau))
            for k in range(3):
                weight[k, x, at, :] = common * channel(v, coef[k])
            totals[pl.ds(b, 1), :] = compact(jnp.sum(tau, axis=1, keepdims=True))

        @pl.loop(1, nd)
        def _(j):
            total_copy(j).start()

    lead_way = (2 * l >= nl).astype(jnp.int32)
    n_lead = hops(lead_way)
    gap = jnp.where(2 * n_lead >= nl - 2, 5, NCH)
    prep_at = jnp.where(n_lead >= 4, 0, NCH)

    @pl.loop(0, 2 * NCH + 1)
    def _(item):
        @pl.when(item == prep_at)
        def _():
            prepare()

        @pl.when(item != prep_at)
        def _():
            k = item - (item > prep_at).astype(jnp.int32)
            both = NCH - gap
            e = k - gap
            mixed = (e >= 0) & (e < 2 * both)
            is_lead = (e < 0) | (mixed & (lax.rem(e + 2 * NCH, 2) == 0))
            half = lax.div(e + 2 * NCH, 2) - NCH
            i = jnp.where(e < 0, k, jnp.where(mixed, jnp.where(is_lead, gap + half, half), e - both))
            way = jnp.where(is_lead, lead_way, 1 - lead_way)
            step(way, i, is_lead)

    @pl.loop(1, nd)
    def _(j):
        peer = lax.rem(d + j, nd)
        wait_recv(gathered.at[peer], r_tot.at[peer])

    gathered[d] = totals[...]
    flip_px = flips[...] != 0
    offset = jnp.zeros((BLOCKS, LANES), f32)
    whole = jnp.zeros((BLOCKS, LANES), f32)
    for src in range(nd):
        got = gathered[src]
        whole = whole + got
        ahead = jnp.where(flip_px, src - d, d - src) > 0
        offset = offset + jnp.where(ahead, got, 0.0)
    through = jnp.exp(-offset)
    totals_scaled = 1.0 - jnp.exp(-whole)

    for b in range(BLOCKS):
        x = b // SL
        y = (b % SL) * LANES
        fwd = lev[0, x, 0, PAD + y + 4 * x : PAD + y + 4 * x + LANES, :]
        z = SL - 1 - x
        bwd = lev[1, z, 0, PAD + y + 4 * z : PAD + y + 4 * z + LANES, :]
        lit = AMBIENT + fwd + bwd
        for k in range(3):
            s = jnp.sum(weight[k, x, y : y + LANES, :] * lit, axis=1, keepdims=True)
            part[b, k : k + 1, :] = compact(s) * through[b : b + 1, :]
        part[b, 3:4, :] = totals_scaled[b : b + 1, :]

    def part_copy(j):
        peer = lax.rem(d + j, nd)
        return pltpu.make_async_remote_copy(
            src_ref=part.at[pl.ds(peer * mine, mine)],
            dst_ref=parts.at[d],
            send_sem=s_part.at[j],
            recv_sem=r_part.at[d],
            device_id=(l, peer),
            device_id_type=MESH,
        )

    @pl.loop(1, nd)
    def _(j):
        part_copy(j).start()

    own = part[pl.ds(d * mine, mine)]
    image = own

    @pl.loop(1, nd)
    def _(j):
        peer = lax.rem(d + j, nd)
        wait_recv(parts.at[peer], r_part.at[peer])

    parts[d] = own
    image = parts[0]
    for src in range(1, nd):
        image = image + parts[src]
    for m in range(mine):
        at = slice(m * LANES, (m + 1) * LANES)
        out[0:3, at] = image[m, 0:3, :]
        out[3:4, at] = own[m, 3:4, :]

    @pl.loop(1, nd)
    def _(j):
        total_copy(j).wait_send()
        part_copy(j).wait_send()

    for side, there in sides:

        @pl.when(there)
        def _():
            @pl.loop(0, NF)
            def _(i):
                fade_copy(side, i).wait_send()

    for way, first in ((0, 0), (1, nl - 1)):
        n = hops(way)
        odd = lax.rem(n, 2)

        @pl.loop(0, NCH)
        def _(i):
            @pl.when((n < nl - 1) & (i >= odd))
            def _():
                main_copy(way, i).wait_send()

            for side, there in sides:

                @pl.when(there & (n < nl - 1) & (lax.rem(n, 4) == 3) & (i >= odd))
                def _():
                    side_copy(way, side, i).wait_send()

                @pl.when(there & (l == first) & (i < NCH - 1))
                def _():
                    source_copy(way, side, i).wait_send()


def solution(mesh):
    nl, nd = mesh.shape["light"], mesh.shape["depth"]
    mine = BLOCKS // nd
    f32 = jnp.float32
    dma = pltpu.SemaphoreType.DMA

    def per_device(density, tf_table, tf_index, light_sources, spread_taps, view_flip):
        vmem = pl.BlockSpec(memory_space=pltpu.VMEM)
        smem = pl.BlockSpec(memory_space=pltpu.SMEM)
        return pl.pallas_call(
            functools.partial(kernel, nl, nd),
            out_shape=jax.ShapeDtypeStruct((4, mine * LANES), f32),
            in_specs=[vmem, smem, smem, vmem, smem, vmem],
            out_specs=vmem,
            scratch_shapes=[
                pltpu.VMEM((2, SL, 2, TALL, LANES), f32),
                pltpu.VMEM((2, 2, TALL, LANES), f32),
                pltpu.VMEM((SL, TALL, LANES), f32),
                pltpu.VMEM((2, SL, TALL, LANES), f32),
                pltpu.VMEM((2, 2, TALL, LANES), f32),
                pltpu.VMEM((3, SL, ROWS, LANES), f32),
                pltpu.VMEM((BLOCKS, LANES), f32),
                pltpu.VMEM((nd, BLOCKS, LANES), f32),
                pltpu.VMEM((BLOCKS, 8, LANES), f32),
                pltpu.VMEM((nd, mine, 8, LANES), f32),
                dma((2, NCH)),
                dma((2, NCH)),
                dma((2, 2, NCH)),
                dma((2, 2, NCH)),
                dma((2, NF)),
                dma((2, NF)),
                dma((nd,)),
                dma((nd,)),
                dma((nd,)),
                dma((nd,)),
            ],
            compiler_params=pltpu.CompilerParams(
                collective_id=0, has_side_effects=True, vmem_limit_bytes=48 << 20
            ),
            name="waves",
        )(density, tf_table, tf_index, light_sources, spread_taps, view_flip.reshape(BLOCKS, LANES))

    return jax.shard_map(
        per_device,
        mesh=mesh,
        in_specs=(
            P("light", None, "depth"),
            P(),
            P("light", "depth"),
            P(None, None, "depth"),
            P(),
            P("light"),
        ),
        out_specs=P(None, ("light", "depth")),
        check_vma=False,
    )
```

time: 1460 us -> 122 us (0.08)
  the two profiles are of different devices: /device:TPU:62 before, /device:TPU:1 now
where the time goes in v1:
time: 122 us
  Pallas kernels  118 us (97%)
  local copies, waits for them, and re-layouts  3.66 us (3%)
    pallas_call x1, Pallas kernels, per_device(): pl.pallas_call(functools.partial(kernel, nl, nd), out_shape=jax.ShapeDtyp...  118 us
    unnamed x10, local copies, waits for them, and re-layouts  3.66 us

profile of v1, /device:TPU:1, one launch (start us, length us, event | category | flops | bytes accessed | tf_op | source)
XLA Modules:
  0.0 122.1 jit_solution(12020927939261179936)
XLA Ops:
  0.7 0.0 copy-start.2
  0.7 0.0 copy-start.3
  0.7 0.8 copy.7.table
  1.5 0.0 copy-done.2
  1.5 0.0 copy-done.3
  1.5 0.0 copy-start
  1.5 1.2 %copy-done = f32[4,512,128]{2,1,0:T(8,128)S(1)} copy-done((f32[4,512,128]{2,1,0:T(8,128)S(1)}, f32[4,512,128]{2,1,0:T(8,128)}, u32[]{:S(2)}) %copy-start) | copy-done | bytes 1048600
  2.7 0.0 copy-start.1
  2.7 1.0 copy-done.1
  3.8 117.7 %waves.1 = f32[4,128]{1,0:T(4,128)S(1)} custom-call(f32[4,512,128]{2,1,0:T(8,128)S(1)} %copy-done, f32[8,4,4]{2,1,0:T(4,128)S(1)} %copy.7.table, s32[1,1]{1,0:T(1,128)S(6)} %copy.9.index, f32[2,512,128]{2,1,0:T(8,128)S(1)} %copy-done.1, f32[9]{0:T(128)S(1)} %copy-done.3, s32[16,128]{1,0:T(8,128)S(1)} %bitcast.1), custom_call_target="tpu_custom_call" | custom-call | tf_op jit(solution)/shard_map/waves/pallas_call | solution.py:451
  121.5 0.6 copy.10
Async XLA Ops:
  0.7 0.8 copy-start.2
  0.7 0.8 copy-start.3
  1.5 1.2 %copy-start = (f32[4,512,128]{2,1,0:T(8,128)S(1)}, f32[4,512,128]{2,1,0:T(8,128)}, u32[]{:S(2)}) copy-start(f32[4,512,128]{2,1,0:T(8,128)} %dens.1) | copy-start | bytes 3145732
  2.7 1.0 copy-start.1

commit v2 on v1

--- a/solution.py
+++ b/solution.py
@@ -39,7 +39,10 @@
     flips,
     out,
     lev,
-    leave,
+    outbox,
+    inbox,
+    side_out,
+    side_in,
     fade,
     fade_nb,
     light_nb,
@@ -90,6 +93,7 @@
                     fade_nb[side, x, at, :] = zeros
                 for way in range(2):
                     light_nb[way, side, at, :] = zeros
+                    side_in[way, side, i, :, :] = zeros[0 : CH // 2]
 
     for way, first in ((0, 0), (1, nl - 1)):
 
@@ -179,19 +183,19 @@
     tap = [(jnp.full((8, LANES), taps[t], f32) / total_vec)[0:1, :] for t in range(9)]
     lane = lax.broadcasted_iota(jnp.int32, (CH, LANES), 1)
     low_half = lane < LANES // 2
+    half_ch = CH // 2
 
     def hops(way):
         return l + way * (nl - 1 - 2 * l)
 
-    def rows_out(way, i):
-        n = hops(way)
-        return pl.ds(pl.multiple_of(PAD - 16 + i * CH - 16 * lax.rem(n, 2), 16), CH)
-
-    def main_copy(way, i):
-        rows = rows_out(way, i)
+    def sizes(n):
+        m = lax.rem(n, 4)
+        return ((CH, m == 3), (2 * CH, m == 0), (CH + CH // 2, (m == 1) | (m == 2)))
+
+    def main_copy(way, i, size):
         return pltpu.make_async_remote_copy(
-            src_ref=leave.at[way, :, rows, :],
-            dst_ref=lev.at[way, 0, :, rows, :],
+            src_ref=outbox.at[way, i, pl.ds(0, size), :],
+            dst_ref=inbox.at[way, i - lax.rem(hops(way), 2), pl.ds(0, size), :],
             send_sem=s_main.at[way, i],
             recv_sem=r_main.at[way, i - lax.rem(hops(way), 2)],
             device_id=(l + 1 - 2 * way, d),
@@ -199,10 +203,9 @@
         )
 
     def side_copy(way, side, i):
-        rows = rows_out(way, i)
         return pltpu.make_async_remote_copy(
-            src_ref=leave.at[way, 0, rows, :],
-            dst_ref=light_nb.at[way, 1 - side, rows, :],
+            src_ref=side_out.at[way, side, i],
+            dst_ref=side_in.at[way, 1 - side, i - 1],
             send_sem=s_nb.at[way, side, i],
             recv_sem=r_nb.at[way, 1 - side, i - 1],
             device_id=(l + 1 - 2 * way, d - 1 + 2 * side),
@@ -225,21 +228,50 @@
                 at = pl.ds(pl.multiple_of(PAD + i * CH, CH), FCH)
                 wait_recv(fade_nb.at[side, :, at, :], r_fade.at[side, lax.div(i, 2)])
 
-        @pl.when((n > 0) & (i < NCH - 1 + odd))
-        def _():
-            wait_recv(lev.at[way, 0, :, rows, :], r_main.at[way, i])
+        for size, sent in sizes(n + 3):
+
+            @pl.when((n > 0) & sent & (i < NCH - 1 + odd))
+            def _():
+                wait_recv(inbox.at[way, i, pl.ds(0, size), :], r_main.at[way, i])
+                lev[way, 0, 0, rows, :] = inbox[way, i, 0:CH, :]
+                if size == 2 * CH:
+                    lev[way, 0, 1, rows, :] = inbox[way, i, CH : 2 * CH, :]
+                elif size > CH:
+                    near = inbox[way, i, CH:size, :]
+                    lev[way, 0, 1, pl.ds(base, half_ch), :] = pltpu.roll(near, 96, 1)
+                    lev[way, 0, 1, pl.ds(base + half_ch, half_ch), :] = pltpu.roll(near, 32, 1)
 
         @pl.when((lax.rem(n, 4) == 0) & (i < NCH - 1))
         def _():
-            for side, there in sides:
-
-                @pl.when(there)
-                def _():
-                    wait_recv(light_nb.at[way, side, rows, :], r_nb.at[way, side, i])
-
-            lev[way, 0, 1, rows, :] = jnp.where(
-                low_half, light_nb[way, 1, rows, :], light_nb[way, 0, rows, :]
-            )
+            @pl.when(n == 0)
+            def _():
+                for side, there in sides:
+
+                    @pl.when(there)
+                    def _():
+                        wait_recv(light_nb.at[way, side, rows, :], r_nb.at[way, side, i])
+
+                lev[way, 0, 1, rows, :] = jnp.where(
+                    low_half, light_nb[way, 1, rows, :], light_nb[way, 0, rows, :]
+                )
+
+            @pl.when(n > 0)
+            def _():
+                for side, there in sides:
+
+                    @pl.when(there)
+                    def _():
+                        wait_recv(side_in.at[way, side, i], r_nb.at[way, side, i])
+
+                lo = side_in[way, 0, i]
+                hi = side_in[way, 1, i]
+                low = low_half[0:half_ch]
+                lev[way, 0, 1, pl.ds(base, half_ch), :] = jnp.where(
+                    low, hi, pltpu.roll(lo, LANES // 2, 1)
+                )
+                lev[way, 0, 1, pl.ds(base + half_ch, half_ch), :] = jnp.where(
+                    low, pltpu.roll(hi, LANES // 2, 1), lo
+                )
 
         for s in range(SL):
             layer = s + way * (SL - 1 - 2 * s)
@@ -269,17 +301,30 @@
                 lev[way, s + 1, 0, rows, :] = sum_a * fade_a
                 lev[way, s + 1, 1, rows, :] = sum_b * fade_b
             else:
-                leave[way, 0, rows_out(way, i), :] = sum_a * fade_a
-                leave[way, 1, rows_out(way, i), :] = sum_b * fade_b
-
-        @pl.when((n < nl - 1) & (i >= odd))
-        def _():
-            main_copy(way, i).start()
-            for side, there in sides:
-
-                @pl.when(there & (lax.rem(n, 4) == 3))
-                def _():
-                    side_copy(way, side, i).start()
+                last_a, last_b = sum_a * fade_a, sum_b * fade_b
+
+        for size, sent in sizes(n):
+
+            @pl.when((n < nl - 1) & sent & (i >= odd))
+            def _():
+                outbox[way, i, 0:CH, :] = last_a
+                low = low_half[0:half_ch]
+                if size == 2 * CH:
+                    outbox[way, i, CH : 2 * CH, :] = last_b
+                elif size > CH:
+                    outbox[way, i, CH:size, :] = jnp.where(
+                        low, pltpu.roll(last_b[0:half_ch], 32, 1), pltpu.roll(last_b[half_ch:CH], 96, 1)
+                    )
+                main_copy(way, i, size).start()
+                if size == CH:
+                    top, bottom = last_a[0:half_ch], last_a[half_ch:CH]
+                    side_out[way, 0, i] = jnp.where(low, top, pltpu.roll(bottom, LANES // 2, 1))
+                    side_out[way, 1, i] = jnp.where(low, pltpu.roll(top, LANES // 2, 1), bottom)
+                    for side, there in sides:
+
+                        @pl.when(there)
+                        def _():
+                            side_copy(way, side, i).start()
 
     row_i = lax.broadcasted_iota(jnp.int32, (LANES, LANES), 0)
     lane_i = lax.broadcasted_iota(jnp.int32, (LANES, LANES), 1)
@@ -424,9 +469,11 @@
 
         @pl.loop(0, NCH)
         def _(i):
-            @pl.when((n < nl - 1) & (i >= odd))
-            def _():
-                main_copy(way, i).wait_send()
+            for size, sent in sizes(n):
+
+                @pl.when((n < nl - 1) & sent & (i >= odd))
+                def _():
+                    main_copy(way, i, size).wait_send()
 
             for side, there in sides:
 
@@ -455,7 +502,10 @@
             out_specs=vmem,
             scratch_shapes=[
                 pltpu.VMEM((2, SL, 2, TALL, LANES), f32),
-                pltpu.VMEM((2, 2, TALL, LANES), f32),
+                pltpu.VMEM((2, NCH, 2 * CH, LANES), f32),
+                pltpu.VMEM((2, NCH, 2 * CH, LANES), f32),
+                pltpu.VMEM((2, 2, NCH, CH // 2, LANES), f32),
+                pltpu.VMEM((2, 2, NCH, CH // 2, LANES), f32),
                 pltpu.VMEM((SL, TALL, LANES), f32),
                 pltpu.VMEM((2, SL, TALL, LANES), f32),
                 pltpu.VMEM((2, 2, TALL, LANES), f32),

time: 122 us -> 116 us (0.951)
  Pallas kernels: 118 us -> 112 us
    pallas_call x1, Pallas kernels: 118 us -> 112 us  [per_device(): pl.pallas_call(functools.partial(kernel, nl, nd), out_shape=jax.ShapeDtyp...]
where the time goes in v2:
time: 116 us
  Pallas kernels  112 us (97%)
  local copies, waits for them, and re-layouts  3.66 us (3%)
    pallas_call x1, Pallas kernels, per_device(): pl.pallas_call(functools.partial(kernel, nl, nd), out_shape=jax.ShapeDtyp...  112 us
    unnamed x10, local copies, waits for them, and re-layouts  3.66 us

profile of v2, /device:TPU:1, one launch (start us, length us, event | category | flops | bytes accessed | tf_op | source)
XLA Modules:
  0.0 116.2 jit_solution(10798771472890358963)
XLA Ops:
  0.7 0.0 copy-start.2
  0.7 0.0 copy-start.3
  0.7 0.8 copy.7.table
  1.5 0.0 copy-done.2
  1.5 0.0 copy-done.3
  1.5 0.0 copy-start
  1.5 1.2 %copy-done = f32[4,512,128]{2,1,0:T(8,128)S(1)} copy-done((f32[4,512,128]{2,1,0:T(8,128)S(1)}, f32[4,512,128]{2,1,0:T(8,128)}, u32[]{:S(2)}) %copy-start) | copy-done | bytes 1048600
  2.7 0.0 copy-start.1
  2.7 1.0 copy-done.1
  3.8 111.8 %waves.1 = f32[4,128]{1,0:T(4,128)S(1)} custom-call(f32[4,512,128]{2,1,0:T(8,128)S(1)} %copy-done, f32[8,4,4]{2,1,0:T(4,128)S(1)} %copy.7.table, s32[1,1]{1,0:T(1,128)S(6)} %copy.9.index, f32[2,512,128]{2,1,0:T(8,128)S(1)} %copy-done.1, f32[9]{0:T(128)S(1)} %copy-done.3, s32[16,128]{1,0:T(8,128)S(1)} %bitcast.1), custom_call_target="tpu_custom_call" | custom-call | tf_op jit(solution)/shard_map/waves/pallas_call | solution.py:498
  115.6 0.6 copy.10
Async XLA Ops:
  0.7 0.8 copy-start.2
  0.7 0.8 copy-start.3
  1.5 1.2 %copy-start = (f32[4,512,128]{2,1,0:T(8,128)S(1)}, f32[4,512,128]{2,1,0:T(8,128)}, u32[]{:S(2)}) copy-start(f32[4,512,128]{2,1,0:T(8,128)} %dens.1) | copy-start | bytes 3145732
  2.7 1.0 copy-start.1

commit v3 on v2

--- a/solution.py
+++ b/solution.py
@@ -31,26 +31,32 @@
 def kernel(
     nl,
     nd,
-    dens,
+    dens_hbm,
     table,
     index,
-    sources,
+    sources_hbm,
     taps,
     flips,
     out,
+    dens,
+    sources,
     lev,
     outbox,
     inbox,
     side_out,
     side_in,
     fade,
-    fade_nb,
+    fade_b,
+    fade_out,
+    fade_in,
     light_nb,
     weight,
     totals,
     gathered,
     part,
     parts,
+    through,
+    alpha,
     s_main,
     r_main,
     s_nb,
@@ -61,13 +67,48 @@
     r_tot,
     s_part,
     r_part,
+    s_dens,
+    s_src,
 ):
     l = lax.axis_index("light")
     d = lax.axis_index("depth")
     has_left = d > 0
     has_right = d < nd - 1
-    mine = BLOCKS // nd
     f32 = jnp.float32
+
+    barrier = pltpu.get_barrier_semaphore()
+
+    def greet(to_l, to_d):
+        pl.semaphore_signal(barrier, 1, device_id=(to_l, to_d), device_id_type=MESH)
+
+    @pl.loop(1, nd)
+    def _(j):
+        greet(l, lax.rem(d + j, nd))
+
+    for dl in (-1, 1):
+        near = (l + dl >= 0) & (l + dl < nl)
+        for dd in (-1, 0, 1):
+
+            @pl.when(near & (d + dd >= 0) & (d + dd < nd))
+            def _():
+                greet(l + dl, d + dd)
+
+    def dens_copy(i):
+        rows = pl.ds(pl.multiple_of(i * FCH, FCH), FCH)
+        return pltpu.make_async_copy(dens_hbm.at[:, rows, :], dens.at[:, rows, :], s_dens.at[i])
+
+    def light_copy(way):
+        return pltpu.make_async_copy(sources_hbm.at[way], sources.at[way], s_src.at[way])
+
+    for way, first in ((0, 0), (1, nl - 1)):
+
+        @pl.when(l == first)
+        def _():
+            light_copy(way).start()
+
+    @pl.loop(0, NF)
+    def _(i):
+        dens_copy(i).start()
 
     zeros = jnp.zeros((PAD, LANES), f32)
     for way in range(2):
@@ -79,9 +120,8 @@
     for x in range(SL):
         fade[x, 0:PAD, :] = zeros
         fade[x, PAD + ROWS : TALL, :] = zeros
-        for side in range(2):
-            fade_nb[side, x, 0:PAD, :] = zeros
-            fade_nb[side, x, PAD + ROWS : TALL, :] = zeros
+        fade_b[x, 0:PAD, :] = zeros
+        fade_b[x, PAD + ROWS : TALL, :] = zeros
     for side, there in ((0, has_left), (1, has_right)):
 
         @pl.when(jnp.logical_not(there))
@@ -90,7 +130,8 @@
             def _(i):
                 at = pl.ds(pl.multiple_of(PAD + i * CH, CH), CH)
                 for x in range(SL):
-                    fade_nb[side, x, at, :] = zeros
+                    part_at = pl.ds(pl.multiple_of(16 * lax.rem(i, 2), 16), 16)
+                    fade_in[side, lax.div(i, 2), x, part_at, :] = zeros[0:16]
                 for way in range(2):
                     light_nb[way, side, at, :] = zeros
                     side_in[way, side, i, :, :] = zeros[0 : CH // 2]
@@ -99,51 +140,32 @@
 
         @pl.when(l == first)
         def _():
+            light_copy(way).wait()
+
             @pl.loop(0, ROWS // CH)
             def _(i):
                 lev[way, 0, 0, pl.ds(pl.multiple_of(PAD + i * CH, CH), CH), :] = sources[
                     way, pl.ds(pl.multiple_of(i * CH, CH), CH), :
                 ]
 
-    barrier = pltpu.get_barrier_semaphore()
-
-    def greet(to_l, to_d):
-        pl.semaphore_signal(barrier, 1, device_id=(to_l, to_d), device_id_type=MESH)
-
-    @pl.loop(1, nd)
-    def _(j):
-        greet(l, lax.rem(d + j, nd))
-
-    for dl in (-1, 1):
-        near = (l + dl >= 0) & (l + dl < nl)
-        for dd in (-1, 0, 1):
-
-            @pl.when(near & (d + dd >= 0) & (d + dd < nd))
-            def _():
-                greet(l + dl, d + dd)
+    lane = lax.broadcasted_iota(jnp.int32, (CH, LANES), 1)
+    low_half = lane < LANES // 2
+    half_ch = CH // 2
 
     k_at = index[0, 0]
     coef = [[table[k_at, k, j] for j in range(4)] for k in range(4)]
     absorb = LIGHT_DEPTH / (SL * nl)
     thick = VIEW_DEPTH / (nd * LANES)
 
-    @pl.loop(0, NF)
-    def _(i):
-        src = pl.ds(pl.multiple_of(i * FCH, FCH), FCH)
-        dst = pl.ds(pl.multiple_of(PAD + i * FCH, 32), FCH)
-        for x in range(SL):
-            fade[x, dst, :] = jnp.exp(-absorb * channel(dens[x, src, :], coef[3]))
-
     beside = (has_left.astype(jnp.int32) + has_right.astype(jnp.int32)) + 1
     lights = (l > 0).astype(jnp.int32) + (l < nl - 1).astype(jnp.int32)
     pl.semaphore_wait(barrier, nd - 1 + lights * beside)
 
     def fade_copy(side, i):
-        rows = pl.ds(pl.multiple_of(PAD + i * FCH, 32), FCH)
         to = d - 1 + 2 * side
         return pltpu.make_async_remote_copy(
-            src_ref=fade.at[:, rows, :],
-            dst_ref=fade_nb.at[1 - side, :, rows, :],
+            src_ref=fade_out.at[side, i],
+            dst_ref=fade_in.at[1 - side, i],
             send_sem=s_fade.at[side, i],
             recv_sem=r_fade.at[1 - side, i],
             device_id=(l, to),
@@ -172,6 +194,17 @@
                     source_copy(way, side, 2 * i).start()
                     source_copy(way, side, 2 * i + 1).start()
 
+        src = pl.ds(pl.multiple_of(i * FCH, FCH), FCH)
+        dst = pl.ds(pl.multiple_of(PAD + i * FCH, 32), FCH)
+        dens_copy(i).wait()
+        for x in range(SL):
+            f = jnp.exp(-absorb * channel(dens[x, src, :], coef[3]))
+            fade[x, dst, :] = f
+            top, bottom = f[0:CH], f[CH:FCH]
+            fade_out[0, i, x] = jnp.where(low_half, top, pltpu.roll(bottom, LANES // 2, 1))
+            fade_out[1, i, x] = jnp.where(low_half, pltpu.roll(top, LANES // 2, 1), bottom)
+        for side, there in sides:
+
             @pl.when(there)
             def _():
                 fade_copy(side, i).start()
@@ -181,9 +214,6 @@
         total_tap = total_tap + taps[t]
     total_vec = jnp.full((8, LANES), total_tap, f32)
     tap = [(jnp.full((8, LANES), taps[t], f32) / total_vec)[0:1, :] for t in range(9)]
-    lane = lax.broadcasted_iota(jnp.int32, (CH, LANES), 1)
-    low_half = lane < LANES // 2
-    half_ch = CH // 2
 
     def hops(way):
         return l + way * (nl - 1 - 2 * l)
@@ -215,18 +245,31 @@
     def wait_recv(dst, sem):
         pltpu.make_async_copy(dst, dst, sem).wait()
 
-    def step(way, i, lead):
+    def receive(way, i, lead):
         n = hops(way)
         odd = lax.rem(n, 2)
         base = pl.multiple_of(PAD + i * CH - 16 * odd, 16)
         rows = pl.ds(base, CH)
 
-        for side, there in sides:
-
-            @pl.when(there & lead & (lax.rem(i, 2) == 0) & (i < 2 * NF))
-            def _():
-                at = pl.ds(pl.multiple_of(PAD + i * CH, CH), FCH)
-                wait_recv(fade_nb.at[side, :, at, :], r_fade.at[side, lax.div(i, 2)])
+        early = (lax.rem(i, 2) == 0) & (i < 2 * NF)
+
+        @pl.when(early & lead)
+        def _():
+            j = lax.div(i, 2)
+            for side, there in sides:
+
+                @pl.when(there)
+                def _():
+                    wait_recv(fade_in.at[side, j], r_fade.at[side, j])
+
+            at = pl.multiple_of(PAD + i * CH, CH)
+            for x in range(SL):
+                lo = fade_in[0, j, x]
+                hi = fade_in[1, j, x]
+                fade_b[x, pl.ds(at, CH), :] = jnp.where(low_half, hi, pltpu.roll(lo, LANES // 2, 1))
+                fade_b[x, pl.ds(at + CH, CH), :] = jnp.where(
+                    low_half, pltpu.roll(hi, LANES // 2, 1), lo
+                )
 
         for size, sent in sizes(n + 3):
 
@@ -273,36 +316,46 @@
                     low, pltpu.roll(hi, LANES // 2, 1), lo
                 )
 
+    def slice_of(way, i, s):
+        odd = lax.rem(hops(way), 2)
+        base = pl.multiple_of(PAD + i * CH - 16 * odd, 16)
+        layer = s + way * (SL - 1 - 2 * s)
+        cols = []
+        for tile in range(2):
+            acc = tap[0] * lev[way, s, tile, pl.ds(base - 8, CH), :]
+            for t in range(1, 9):
+                acc = acc + tap[t] * lev[way, s, tile, pl.ds(base - 8 + t, CH), :]
+            cols.append(acc)
+        a, b = cols
+        sum_a, sum_b = tap[4] * a, tap[4] * b
+        for t in range(9):
+            by = t - 4
+            if by == 0:
+                continue
+            ra = pltpu.roll(a, (-by) % LANES, 1)
+            rb = pltpu.roll(b, (-by) % LANES, 1)
+            own = lane < LANES - by if by > 0 else lane >= -by
+            sum_a = sum_a + tap[t] * jnp.where(own, ra, rb)
+            sum_b = sum_b + tap[t] * jnp.where(own, rb, ra)
+        there_rows = pl.ds(base - 4 * (s + 1), CH)
+        fade_far = fade_b[layer, there_rows, :]
+        return sum_a * fade[layer, there_rows, :], sum_b * fade_far
+
+    def work(*chunks):
         for s in range(SL):
-            layer = s + way * (SL - 1 - 2 * s)
-            cols = []
-            for tile in range(2):
-                acc = tap[0] * lev[way, s, tile, pl.ds(base - 8, CH), :]
-                for t in range(1, 9):
-                    acc = acc + tap[t] * lev[way, s, tile, pl.ds(base - 8 + t, CH), :]
-                cols.append(acc)
-            a, b = cols
-            sum_a, sum_b = tap[4] * a, tap[4] * b
-            for t in range(9):
-                by = t - 4
-                if by == 0:
-                    continue
-                ra = pltpu.roll(a, (-by) % LANES, 1)
-                rb = pltpu.roll(b, (-by) % LANES, 1)
-                own = lane < LANES - by if by > 0 else lane >= -by
-                sum_a = sum_a + tap[t] * jnp.where(own, ra, rb)
-                sum_b = sum_b + tap[t] * jnp.where(own, rb, ra)
-            there_rows = pl.ds(base - 4 * (s + 1), CH)
-            fade_a = fade[layer, there_rows, :]
-            fade_b = jnp.where(
-                low_half, fade_nb[1, layer, there_rows, :], fade_nb[0, layer, there_rows, :]
-            )
+            got = [slice_of(way, i, s) for way, i in chunks]
             if s < SL - 1:
-                lev[way, s + 1, 0, rows, :] = sum_a * fade_a
-                lev[way, s + 1, 1, rows, :] = sum_b * fade_b
-            else:
-                last_a, last_b = sum_a * fade_a, sum_b * fade_b
-
+                for (way, i), (new_a, new_b) in zip(chunks, got):
+                    odd = lax.rem(hops(way), 2)
+                    rows = pl.ds(pl.multiple_of(PAD + i * CH - 16 * odd, 16), CH)
+                    lev[way, s + 1, 0, rows, :] = new_a
+                    lev[way, s + 1, 1, rows, :] = new_b
+        for (way, i), (last_a, last_b) in zip(chunks, got):
+            send(way, i, last_a, last_b)
+
+    def send(way, i, last_a, last_b):
+        n = hops(way)
+        odd = lax.rem(n, 2)
         for size, sent in sizes(n):
 
             @pl.when((n < nl - 1) & sent & (i >= odd))
@@ -366,94 +419,105 @@
         def _(j):
             total_copy(j).start()
 
-    lead_way = (2 * l >= nl).astype(jnp.int32)
-    n_lead = hops(lead_way)
-    gap = jnp.where(2 * n_lead >= nl - 2, 5, NCH)
-    prep_at = jnp.where(n_lead >= 4, 0, NCH)
-
-    @pl.loop(0, 2 * NCH + 1)
-    def _(item):
-        @pl.when(item == prep_at)
-        def _():
-            prepare()
-
-        @pl.when(item != prep_at)
-        def _():
-            k = item - (item > prep_at).astype(jnp.int32)
-            both = NCH - gap
-            e = k - gap
-            mixed = (e >= 0) & (e < 2 * both)
-            is_lead = (e < 0) | (mixed & (lax.rem(e + 2 * NCH, 2) == 0))
-            half = lax.div(e + 2 * NCH, 2) - NCH
-            i = jnp.where(e < 0, k, jnp.where(mixed, jnp.where(is_lead, gap + half, half), e - both))
-            way = jnp.where(is_lead, lead_way, 1 - lead_way)
-            step(way, i, is_lead)
-
-    @pl.loop(1, nd)
-    def _(j):
-        peer = lax.rem(d + j, nd)
-        wait_recv(gathered.at[peer], r_tot.at[peer])
-
-    gathered[d] = totals[...]
-    flip_px = flips[...] != 0
-    offset = jnp.zeros((BLOCKS, LANES), f32)
-    whole = jnp.zeros((BLOCKS, LANES), f32)
-    for src in range(nd):
-        got = gathered[src]
-        whole = whole + got
-        ahead = jnp.where(flip_px, src - d, d - src) > 0
-        offset = offset + jnp.where(ahead, got, 0.0)
-    through = jnp.exp(-offset)
-    totals_scaled = 1.0 - jnp.exp(-whole)
-
-    for b in range(BLOCKS):
-        x = b // SL
-        y = (b % SL) * LANES
-        fwd = lev[0, x, 0, PAD + y + 4 * x : PAD + y + 4 * x + LANES, :]
-        z = SL - 1 - x
-        bwd = lev[1, z, 0, PAD + y + 4 * z : PAD + y + 4 * z + LANES, :]
-        lit = AMBIENT + fwd + bwd
-        for k in range(3):
-            s = jnp.sum(weight[k, x, y : y + LANES, :] * lit, axis=1, keepdims=True)
-            part[b, k : k + 1, :] = compact(s) * through[b : b + 1, :]
-        part[b, 3:4, :] = totals_scaled[b : b + 1, :]
-
-    def part_copy(j):
-        peer = lax.rem(d + j, nd)
+    def offsets():
+        @pl.loop(1, nd)
+        def _(j):
+            peer = lax.rem(d + j, nd)
+            wait_recv(gathered.at[peer], r_tot.at[peer])
+
+        gathered[d] = totals[...]
+        flip_px = flips[...] != 0
+        offset = jnp.zeros((BLOCKS, LANES), f32)
+        whole = jnp.zeros((BLOCKS, LANES), f32)
+        for src in range(nd):
+            got = gathered[src]
+            whole = whole + got
+            ahead = jnp.where(flip_px, src - d, d - src) > 0
+            offset = offset + jnp.where(ahead, got, 0.0)
+        through[...] = jnp.exp(-offset)
+        alpha[...] = 1.0 - jnp.exp(-whole)
+
+    def part_copy(peer):
         return pltpu.make_async_remote_copy(
-            src_ref=part.at[pl.ds(peer * mine, mine)],
-            dst_ref=parts.at[d],
-            send_sem=s_part.at[j],
+            src_ref=part.at[peer, 0:4],
+            dst_ref=parts.at[d, 0:4],
+            send_sem=s_part.at[peer],
             recv_sem=r_part.at[d],
             device_id=(l, peer),
             device_id_type=MESH,
         )
 
-    @pl.loop(1, nd)
-    def _(j):
-        part_copy(j).start()
-
-    own = part[pl.ds(d * mine, mine)]
-    image = own
+    def finish(g):
+        y = pl.multiple_of(g * LANES, LANES)
+        for x in range(SL):
+            b = x * (ROWS // LANES) + g
+            z = SL - 1 - x
+            fwd = lev[0, x, 0, pl.ds(PAD + 4 * x + y, LANES), :]
+            bwd = lev[1, z, 0, pl.ds(PAD + 4 * z + y, LANES), :]
+            lit = AMBIENT + fwd + bwd
+            for k in range(3):
+                s = jnp.sum(weight[k, x, pl.ds(y, LANES), :] * lit, axis=1, keepdims=True)
+                part[b, k : k + 1, :] = compact(s) * through[pl.ds(b, 1), :]
+
+            @pl.when(b != d)
+            def _():
+                part_copy(b).start()
+
+    lead_way = (2 * l >= nl).astype(jnp.int32)
+    n_lead = hops(lead_way)
+    gap = jnp.where(2 * n_lead >= nl - 2, 8, NCH)
+    prep_at = jnp.where(n_lead >= 4, 0, NCH)
+
+    @pl.loop(0, 2 * NCH + 1)
+    def _(item):
+        @pl.when(item == prep_at)
+        def _():
+            prepare()
+
+        @pl.when(item != prep_at)
+        def _():
+            k = item - (item > prep_at).astype(jnp.int32)
+            e = k - gap
+            first_on = k < NCH
+            second_on = (e >= 0) & (e < NCH)
+
+            @pl.when(e == 0)
+            def _():
+                offsets()
+
+            @pl.when(first_on & second_on)
+            def _():
+                receive(lead_way, k, True)
+                receive(1 - lead_way, e, False)
+                work((lead_way, k), (1 - lead_way, e))
+
+            @pl.when(first_on != second_on)
+            def _():
+                i = jnp.where(first_on, k, e)
+                way = jnp.where(first_on, lead_way, 1 - lead_way)
+                receive(way, i, first_on)
+                work((way, i))
+
+            @pl.when(second_on & (e > 0) & (lax.rem(e, 4) == 0))
+            def _():
+                finish(lax.div(e, 4) - 1)
 
     @pl.loop(1, nd)
     def _(j):
         peer = lax.rem(d + j, nd)
-        wait_recv(parts.at[peer], r_part.at[peer])
-
-    parts[d] = own
+        wait_recv(parts.at[peer, 0:4], r_part.at[peer])
+
+    parts[d] = part[d]
     image = parts[0]
     for src in range(1, nd):
         image = image + parts[src]
-    for m in range(mine):
-        at = slice(m * LANES, (m + 1) * LANES)
-        out[0:3, at] = image[m, 0:3, :]
-        out[3:4, at] = own[m, 3:4, :]
+    out[0:3, :] = image[0:3, :]
+    out[3:4, :] = alpha[pl.ds(d, 1), :]
 
     @pl.loop(1, nd)
     def _(j):
         total_copy(j).wait_send()
-        part_copy(j).wait_send()
+        part_copy(lax.rem(d + j, nd)).wait_send()
 
     for side, there in sides:
 
@@ -494,26 +558,33 @@
 
     def per_device(density, tf_table, tf_index, light_sources, spread_taps, view_flip):
         vmem = pl.BlockSpec(memory_space=pltpu.VMEM)
+        anywhere = pl.BlockSpec(memory_space=pl.ANY)
         smem = pl.BlockSpec(memory_space=pltpu.SMEM)
         return pl.pallas_call(
             functools.partial(kernel, nl, nd),
             out_shape=jax.ShapeDtypeStruct((4, mine * LANES), f32),
-            in_specs=[vmem, smem, smem, vmem, smem, vmem],
+            in_specs=[anywhere, smem, smem, anywhere, smem, vmem],
             out_specs=vmem,
             scratch_shapes=[
+                pltpu.VMEM((SL, ROWS, LANES), f32),
+                pltpu.VMEM((2, ROWS, LANES), f32),
                 pltpu.VMEM((2, SL, 2, TALL, LANES), f32),
                 pltpu.VMEM((2, NCH, 2 * CH, LANES), f32),
                 pltpu.VMEM((2, NCH, 2 * CH, LANES), f32),
                 pltpu.VMEM((2, 2, NCH, CH // 2, LANES), f32),
                 pltpu.VMEM((2, 2, NCH, CH // 2, LANES), f32),
                 pltpu.VMEM((SL, TALL, LANES), f32),
-                pltpu.VMEM((2, SL, TALL, LANES), f32),
+                pltpu.VMEM((SL, TALL, LANES), f32),
+                pltpu.VMEM((2, NF, SL, CH, LANES), f32),
+                pltpu.VMEM((2, NF, SL, CH, LANES), f32),
                 pltpu.VMEM((2, 2, TALL, LANES), f32),
                 pltpu.VMEM((3, SL, ROWS, LANES), f32),
                 pltpu.VMEM((BLOCKS, LANES), f32),
                 pltpu.VMEM((nd, BLOCKS, LANES), f32),
                 pltpu.VMEM((BLOCKS, 8, LANES), f32),
-                pltpu.VMEM((nd, mine, 8, LANES), f32),
+                pltpu.VMEM((nd, 8, LANES), f32),
+                pltpu.VMEM((BLOCKS, LANES), f32),
+                pltpu.VMEM((BLOCKS, LANES), f32),
                 dma((2, NCH)),
                 dma((2, NCH)),
                 dma((2, 2, NCH)),
@@ -524,6 +595,8 @@
                 dma((nd,)),
                 dma((nd,)),
                 dma((nd,)),
+                dma((NF,)),
+                dma((2,)),
             ],
             compiler_params=pltpu.CompilerParams(
                 collective_id=0, has_side_effects=True, vmem_limit_bytes=48 << 20

time: 116 us -> 111 us (0.957)
  the two profiles are of different devices: /device:TPU:1 before, /device:TPU:33 now
where the time goes in v3:
time: 111 us
  Pallas kernels  106 us (95%)
  local copies, waits for them, and re-layouts  3.66 us (3%)
    pallas_call x1, Pallas kernels, per_device(): pl.pallas_call(functools.partial(kernel, nl, nd), out_shape=jax.ShapeDtyp...  106 us
    unnamed x10, local copies, waits for them, and re-layouts  3.66 us

profile of v3, /device:TPU:33, one launch (start us, length us, event | category | flops | bytes accessed | tf_op | source)
XLA Modules:
  0.0 110.6 jit_solution(6927576554566273179)
XLA Ops:
  0.7 0.0 copy-start.2
  0.7 0.0 copy-start.3
  0.7 0.8 copy.7.table
  1.5 0.0 copy-done.2
  1.5 0.0 copy-done.3
  1.5 0.0 copy-start
  1.5 1.2 %copy-done = f32[4,512,128]{2,1,0:T(8,128)S(1)} copy-done((f32[4,512,128]{2,1,0:T(8,128)S(1)}, f32[4,512,128]{2,1,0:T(8,128)}, u32[]{:S(2)}) %copy-start) | copy-done | bytes 1048600
  2.7 0.0 copy-start.1
  2.7 1.0 copy-done.1
  3.8 106.3 %waves.1 = f32[4,128]{1,0:T(4,128)S(1)} custom-call(f32[4,512,128]{2,1,0:T(8,128)S(1)} %copy-done, f32[8,4,4]{2,1,0:T(4,128)S(1)} %copy.7.table, s32[1,1]{1,0:T(1,128)S(6)} %copy.9.index, f32[2,512,128]{2,1,0:T(8,128)S(1)} %copy-done.1, f32[9]{0:T(128)S(1)} %copy-done.3, s32[16,128]{1,0:T(8,128)S(1)} %bitcast.1), custom_call_target="tpu_custom_call" | custom-call | tf_op jit(solution)/shard_map/waves/pallas_call | solution.py:563
  110.0 0.6 copy.10
Async XLA Ops:
  0.7 0.8 copy-start.2
  0.7 0.8 copy-start.3
  1.5 1.2 %copy-start = (f32[4,512,128]{2,1,0:T(8,128)S(1)}, f32[4,512,128]{2,1,0:T(8,128)}, u32[]{:S(2)}) copy-start(f32[4,512,128]{2,1,0:T(8,128)} %dens_hbm.1) | copy-start | bytes 3145732
  2.7 1.0 copy-start.1

commit v4 on v3

--- a/solution.py
+++ b/solution.py
@@ -316,16 +316,20 @@
                     low, pltpu.roll(hi, LANES // 2, 1), lo
                 )
 
+    def added(terms):
+        while len(terms) > 1:
+            terms = [sum(terms[j + 1 : j + 2], terms[j]) for j in range(0, len(terms), 2)]
+        return terms[0]
+
     def slice_of(way, i, s):
         odd = lax.rem(hops(way), 2)
         base = pl.multiple_of(PAD + i * CH - 16 * odd, 16)
         layer = s + way * (SL - 1 - 2 * s)
         cols = []
         for tile in range(2):
-            acc = tap[0] * lev[way, s, tile, pl.ds(base - 8, CH), :]
-            for t in range(1, 9):
-                acc = acc + tap[t] * lev[way, s, tile, pl.ds(base - 8 + t, CH), :]
-            cols.append(acc)
+            cols.append(
+                added([tap[t] * lev[way, s, tile, pl.ds(base - 8 + t, CH), :] for t in range(9)])
+            )
         a, b = cols
         sum_a, sum_b = tap[4] * a, tap[4] * b
         for t in range(9):

time: 111 us -> 110 us (level)
  no operation moved by 1% of the time
where the time goes in v4:
time: 110 us
  Pallas kernels  106 us (96%)
  local copies, waits for them, and re-layouts  3.66 us (3%)
    pallas_call x1, Pallas kernels, per_device(): pl.pallas_call(functools.partial(kernel, nl, nd), out_shape=jax.ShapeDtyp...  106 us
    unnamed x10, local copies, waits for them, and re-layouts  3.66 us

profile of v4, /device:TPU:33, one launch (start us, length us, event | category | flops | bytes accessed | tf_op | source)
XLA Modules:
  0.0 110.1 jit_solution(10210342623834753709)
XLA Ops:
  0.7 0.0 copy-start.2
  0.7 0.0 copy-start.3
  0.7 0.8 copy.7.table
  1.5 0.0 copy-done.2
  1.5 0.0 copy-done.3
  1.5 0.0 copy-start
  1.5 1.2 %copy-done = f32[4,512,128]{2,1,0:T(8,128)S(1)} copy-done((f32[4,512,128]{2,1,0:T(8,128)S(1)}, f32[4,512,128]{2,1,0:T(8,128)}, u32[]{:S(2)}) %copy-start) | copy-done | bytes 1048600
  2.7 0.0 copy-start.1
  2.7 1.0 copy-done.1
  3.8 105.7 %waves.1 = f32[4,128]{1,0:T(4,128)S(1)} custom-call(f32[4,512,128]{2,1,0:T(8,128)S(1)} %copy-done, f32[8,4,4]{2,1,0:T(4,128)S(1)} %copy.7.table, s32[1,1]{1,0:T(1,128)S(6)} %copy.9.index, f32[2,512,128]{2,1,0:T(8,128)S(1)} %copy-done.1, f32[9]{0:T(128)S(1)} %copy-done.3, s32[16,128]{1,0:T(8,128)S(1)} %bitcast.1), custom_call_target="tpu_custom_call" | custom-call | tf_op jit(solution)/shard_map/waves/pallas_call | solution.py:567
  109.5 0.6 copy.10
Async XLA Ops:
  0.7 0.8 copy-start.2
  0.7 0.8 copy-start.3
  1.5 1.2 %copy-start = (f32[4,512,128]{2,1,0:T(8,128)S(1)}, f32[4,512,128]{2,1,0:T(8,128)}, u32[]{:S(2)}) copy-start(f32[4,512,128]{2,1,0:T(8,128)} %dens_hbm.1) | copy-start | bytes 3145732
  2.7 1.0 copy-start.1

commit v5 on v4

--- a/solution.py
+++ b/solution.py
@@ -212,8 +212,8 @@
     total_tap = taps[0]
     for t in range(1, 9):
         total_tap = total_tap + taps[t]
-    total_vec = jnp.full((8, LANES), total_tap, f32)
-    tap = [(jnp.full((8, LANES), taps[t], f32) / total_vec)[0:1, :] for t in range(9)]
+    total_vec = jnp.full((CH, LANES), total_tap, f32)
+    tap = [jnp.full((CH, LANES), taps[t], f32) / total_vec for t in range(9)]
 
     def hops(way):
         return l + way * (nl - 1 - 2 * l)

time: 110 us -> 110 us (level)
  no operation moved by 1% of the time
where the time goes in v5:
time: 110 us
  Pallas kernels  106 us (96%)
  local copies, waits for them, and re-layouts  3.66 us (3%)
    pallas_call x1, Pallas kernels, per_device(): pl.pallas_call(functools.partial(kernel, nl, nd), out_shape=jax.ShapeDtyp...  106 us
    unnamed x10, local copies, waits for them, and re-layouts  3.66 us

profile of v5, /device:TPU:33, one launch (start us, length us, event | category | flops | bytes accessed | tf_op | source)
XLA Modules:
  0.0 110.1 jit_solution(10210342623834753709)
XLA Ops:
  0.7 0.0 copy-start.2
  0.7 0.0 copy-start.3
  0.7 0.8 copy.7.table
  1.5 0.0 copy-done.2
  1.5 0.0 copy-done.3
  1.5 0.0 copy-start
  1.5 1.2 %copy-done = f32[4,512,128]{2,1,0:T(8,128)S(1)} copy-done((f32[4,512,128]{2,1,0:T(8,128)S(1)}, f32[4,512,128]{2,1,0:T(8,128)}, u32[]{:S(2)}) %copy-start) | copy-done | bytes 1048600
  2.7 0.0 copy-start.1
  2.7 1.0 copy-done.1
  3.8 105.7 %waves.1 = f32[4,128]{1,0:T(4,128)S(1)} custom-call(f32[4,512,128]{2,1,0:T(8,128)S(1)} %copy-done, f32[8,4,4]{2,1,0:T(4,128)S(1)} %copy.7.table, s32[1,1]{1,0:T(1,128)S(6)} %copy.9.index, f32[2,512,128]{2,1,0:T(8,128)S(1)} %copy-done.1, f32[9]{0:T(128)S(1)} %copy-done.3, s32[16,128]{1,0:T(8,128)S(1)} %bitcast.1), custom_call_target="tpu_custom_call" | custom-call | tf_op jit(solution)/shard_map/waves/pallas_call | solution.py:567
  109.5 0.6 copy.10
Async XLA Ops:
  0.7 0.8 copy-start.2
  0.7 0.8 copy-start.3
  1.5 1.2 %copy-start = (f32[4,512,128]{2,1,0:T(8,128)S(1)}, f32[4,512,128]{2,1,0:T(8,128)}, u32[]{:S(2)}) copy-start(f32[4,512,128]{2,1,0:T(8,128)} %dens_hbm.1) | copy-start | bytes 3145732
  2.7 1.0 copy-start.1
